TPU v7x, 32 devices: a whole 2x2x4 slice. The times are simulated.
32 devices in a mesh: rcv: 4 (over z), src: 8 (over y, x, core).
Axes of the slice: x: 2, y: 2, z: 4, core: 2. Of those that a mesh axis runs over, the one named last changes fastest.
Arguments:
- reflection: bfloat16 [2, 16384, 16384], P(None, 'rcv', 'src'), may hold values from -6 to 6
- green: bfloat16 [2, 16384, 512], P(None, 'rcv', 'src'), may hold values from -0.046875 to 0.046875
- tile_mask: int32 [64, 64], replicated, may hold values from 0 to 1, as said below
- reference_index: int32 [512], P(('rcv', 'src')), may hold values from 0 to 511
Outputs:
- aligned: float32 [512, 2, 512], P(('rcv', 'src'))
Inputs may be any that keep to these rules, and one draw needn't show every extreme that they name: `tile_mask`: entries below the diagonal are 0.
All inputs are finite; a program needn't handle non-finite values.
Results may differ from a plain program's by a relative error of at most 0.02.
Values may be sent and summed in bfloat16 or wider, within the bound.
A program may use at most 256 MiB of HBM per device.

v0:
```python
import jax
import jax.numpy as jnp
from jax import lax
from jax.sharding import PartitionSpec as P

P_SIZE = 512
TILE = 256


def broadcast(block, axis, holder):
    block = jnp.where(lax.axis_index(axis) == holder, block, jnp.zeros_like(block))
    return lax.psum(block, axis)


def across(first, second, precision=None):
    return lax.dot_general(
        first,
        second,
        (((0,), (0,)), ((), ())),
        precision=precision,
        preferred_element_type=jnp.float32,
    )


def body(reflection, green, tile_mask, reference_index):
    rows_blk = reflection.shape[1]
    col_count = reflection.shape[2]
    rcv_index = lax.axis_index("rcv")
    src_index = lax.axis_index("src")
    green_block = lax.all_gather(green, "src", axis=2, tiled=True)
    src_per_rcv = lax.axis_size("src") // lax.axis_size("rcv")
    green_piece = lax.dynamic_slice_in_dim(
        green_block, src_index % src_per_rcv * col_count, col_count, 1
    )
    green_src = broadcast(green_piece, "rcv", src_index // src_per_rcv)
    row_tiles_count = rows_blk // TILE
    col_tiles_count = col_count // TILE
    tile_block = lax.dynamic_slice(
        tile_mask,
        (rcv_index * row_tiles_count, src_index * col_tiles_count),
        (row_tiles_count, col_tiles_count),
    )
    row_ids = rcv_index * row_tiles_count + jnp.arange(row_tiles_count)
    col_ids = src_index * col_tiles_count + jnp.arange(col_tiles_count)
    kept_tiles = tile_block == 1
    off_diag = kept_tiles & (row_ids[:, None] != col_ids[None, :])
    shaped = reflection.reshape(2, row_tiles_count, TILE, col_tiles_count, TILE)
    zero_value = jnp.zeros((), jnp.bfloat16)
    acquired = jnp.where(kept_tiles[None, :, None, :, None], shaped, zero_value).reshape(
        2, rows_blk, col_count
    )
    mirror_part = jnp.where(off_diag[None, :, None, :, None], shaped, zero_value).reshape(
        2, rows_blk, col_count
    )
    data_wide = jnp.concatenate([acquired[0], acquired[1], mirror_part[0], mirror_part[1]], axis=1)
    green_wide = jnp.concatenate([green_block[0], green_block[1]], axis=1)
    products = across(data_wide, green_wide)

    def quarter(row_slot, col_slot):
        return products[
            row_slot * col_count : (row_slot + 1) * col_count,
            col_slot * P_SIZE : (col_slot + 1) * P_SIZE,
        ]

    front_real = (quarter(0, 0) + quarter(1, 1)).astype(jnp.bfloat16)
    front_imag = (quarter(1, 0) - quarter(0, 1)).astype(jnp.bfloat16)
    back_real = (quarter(2, 0) - quarter(3, 1)).astype(jnp.bfloat16)
    back_imag = (quarter(3, 0) + quarter(2, 1)).astype(jnp.bfloat16)
    src_real = green_src[0]
    src_imag = green_src[1]
    green_stack = jnp.concatenate([src_real, src_imag], axis=0)
    mirror_left = jnp.concatenate(
        [
            jnp.concatenate([back_real, back_imag], axis=1),
            jnp.concatenate([back_imag, -back_real], axis=1),
        ],
        axis=0,
    )
    mirrored = across(green_stack, mirror_left)
    weights = jnp.concatenate(
        [
            jnp.concatenate([src_real, src_imag], axis=1),
            jnp.concatenate([-src_imag, src_real], axis=1),
        ],
        axis=0,
    )
    left_rows = jnp.concatenate([front_real, front_imag], axis=0)
    combined = across(left_rows, weights) + mirrored
    focal = lax.psum_scatter(combined, ("rcv", "src"), scatter_dimension=0, tiled=True)
    focal_real = focal[:, :P_SIZE]
    focal_imag = focal[:, P_SIZE:]
    chosen = jnp.arange(P_SIZE)[None, :] == reference_index[:, None]
    anchor_real = jnp.sum(jnp.where(chosen, focal_real, 0.0), axis=1)[:, None]
    anchor_imag = jnp.sum(jnp.where(chosen, focal_imag, 0.0), axis=1)[:, None]
    out_real = focal_real * anchor_real + focal_imag * anchor_imag
    out_imag = focal_imag * anchor_real - focal_real * anchor_imag
    return jnp.stack([out_real, out_imag], axis=1)


def solution(mesh):
    return jax.shard_map(
        body,
        mesh=mesh,
        in_specs=(P(None, "rcv", "src"), P(None, "rcv", "src"), P(), P(("rcv", "src"))),
        out_specs=P(("rcv", "src"), None, None),
        check_vma=False,
    )
```

profile of v0, /device:TPU:0, one launch (start us, length us, event | category | flops | bytes accessed | tf_op | source)
XLA Modules:
  0.0 491.1 jit_solution(2847651224598530955)
XLA Ops:
  6.5 0.0 all-gather.2.cloned.1.call-start
  6.5 0.7 all-gather.2.cloned.1.call-update
  7.3 0.0 all-reduce.2.cloned.1.call-start
  7.3 23.6 %copy.6 = bf16[1024,8,8,256]{3,2,1,0:T(8,128)(2,1)} copy(bf16[1024,8,8,256]{3,1,2,0:T(8,128)(2,1)} %bitcast.37) | data formatting | bytes 67108864
  30.9 0.8 compare_and_fusion
  31.7 32.3 %broadcast_select_fusion.1 = (bf16[2,16,256,8,256]{4,3,2,1,0:T(8,128)(2,1)}, bf16[2,16,256,8,256]{4,3,2,1,0:T(8,128)(2,1)}) fusion(bf16[2,16,256,8,256]{4,3,2,1,0:T(8,128)(2,1)} %bitcast.30, pred[16,8]{1,0:T(8,128)(4,1)S(1)} %get-tuple-element.10, pred[16,8]{1,0:T(8,128)(4,1)S(1)} %get-tuple-element.9), kind=kLoop, calls=%fused_computation.9 | loop fusion | flops 33554432 | bytes 100663552 | tf_op jit(solution)/shard_map/jit(_where)/select_n | solution.py:49
  64.0 38.8 %fusion.48 = (bf16[1,16,256,8,256]{4,3,2,1,0:T(8,128)(2,1)}, bf16[1,16,256,8,256]{4,3,2,1,0:T(8,128)(2,1)}, bf16[1,16,256,8,256]{4,3,2,1,0:T(8,128)(2,1)S(1)}, bf16[1,16,256,8,256]{4,3,2,1,0:T(8,128)(2,1)}) fusion(bf16[2,16,256,8,256]{4,3,2,1,0:T(8,128)(2,1)} %get-tuple-element.16, bf16[2,16,256,8,256]{4,3,2,1,0:T(8,128)(2,1)} %get-tuple-element.17), kind=kLoop, calls=%fused_computation.64 | loop fusion | bytes 134217728 | tf_op jit(solution)/shard_map/slice | solution.py:55
  102.8 16.3 %copy.7 = bf16[512,8,8,256]{3,1,2,0:T(8,128)(2,1)} copy(bf16[512,8,8,256]{3,2,1,0:T(8,128)(2,1)} %bitcast.36) | data formatting | bytes 33554432
  119.0 0.0 slice-start
  119.0 0.0 slice-start.1
  119.0 0.0 slice-start.2
  119.0 0.0 slice-start.3
  119.0 18.0 %copy.8 = bf16[512,8,8,256]{3,1,2,0:T(8,128)(2,1)} copy(bf16[512,8,8,256]{3,2,1,0:T(8,128)(2,1)} %bitcast.35) | data formatting | bytes 33554432
  137.1 0.0 slice-done
  137.1 0.0 slice-done.1
  137.1 0.0 slice-done.2
  137.1 0.0 slice-done.3
  137.1 9.8 %copy.9 = bf16[512,8,8,256]{3,1,2,0:T(8,128)(2,1)} copy(bf16[512,8,8,256]{3,2,1,0:T(8,128)(2,1)S(1)} %bitcast.34) | data formatting | bytes 33554432
  146.8 9.7 %copy.10 = bf16[512,8,8,256]{3,1,2,0:T(8,128)(2,1)} copy(bf16[512,8,8,256]{3,2,1,0:T(8,128)(2,1)S(1)} %bitcast.31) | data formatting | bytes 33554432
  156.6 0.0 all-gather.2.cloned.1.call-done
  156.6 5.6 %dynamic-slice_select_fusion = bf16[2,2048,512]{1,2,0:T(8,128)(2,1)} fusion(bf16[2,4096,512]{1,2,0:T(8,128)(2,1)} %all-gather.2.cloned.1.call-done, s32[]{:T(128)S(6)} %select_n.49, pred[]{:T(512)S(6)} %eq.26), kind=kLoop, calls=%fused_computation.45 | loop fusion | flops 2097152 | bytes 8388613 | tf_op jit(solution)/shard_map/jit(_where)/select_n | solution.py:11
  162.1 0.0 all-reduce.2.cloned.1.call-update
  162.1 0.2 reduce-scatter.2.cloned.1.call-start
  162.4 6.0 %slice_bitcast_fusion.1 = (bf16[4096,512]{0,1:T(8,128)(2,1)}, bf16[4096,512]{0,1:T(8,128)(2,1)}) fusion(bf16[2,4096,512]{1,2,0:T(8,128)(2,1)} %all-gather.2.cloned.1.call-done), kind=kLoop, calls=%fused_computation.38 | loop fusion | bytes 16777216 | tf_op jit(solution)/shard_map/squeeze | solution.py:56
  168.3 107.8 %fusion = f32[8192,1024]{0,1:T(8,128)} fusion(bf16[4096,2048]{1,0:T(8,128)(2,1)} %bitcast.41, bf16[4096,2048]{1,0:T(8,128)(2,1)} %bitcast.40, bf16[4096,2048]{1,0:T(8,128)(2,1)} %bitcast.39, bf16[4096,2048]{1,0:T(8,128)(2,1)} %bitcast.38, bf16[4096,512]{0,1:T(8,128)(2,1)} %get-tuple-element.21, bf16[4096,512]{0,1:T(8,128)(2,1)} %get-tuple-element.20), kind=kOutput, calls=%fused_computation | convolution fusion | flops 69004689408 | bytes 109051904 | tf_op jit(solution)/shard_map/dot_general | solution.py:16
  276.1 6.0 %fusion.46 = (bf16[2048,512]{0,1:T(8,128)(2,1)S(1)}, bf16[2048,512]{0,1:T(8,128)(2,1)}) fusion(f32[8192,1024]{0,1:T(8,128)} %fusion), kind=kLoop, calls=%fused_computation.63 | loop fusion | flops 3145728 | bytes 12582912 | tf_op jit(solution)/shard_map/neg | solution.py:75
  282.1 11.8 %fusion.27 = (bf16[2048,512]{0,1:T(8,128)(2,1)}, bf16[2048,512]{0,1:T(8,128)(2,1)}, bf16[2048,512]{0,1:T(8,128)(2,1)}) fusion(f32[8192,1024]{0,1:T(8,128)} %fusion), kind=kLoop, calls=%fused_computation.30 | loop fusion | flops 6291456 | bytes 31457280 | tf_op jit(solution)/shard_map/convert_element_type | solution.py:68
  293.9 25.8 %all-reduce.2.cloned.1.call-done = bf16[2,2048,512]{1,2,0:T(8,128)(2,1)} async-done(((bf16[2,2048,512]{1,2,0:T(8,128)(2,1)}), bf16[2,2048,512]{1,2,0:T(8,128)(2,1)}) %all-reduce.2.cloned.1.call-update) | async-done | bytes 4194320 | tf_op jit(solution)/shard_map/psum | solution.py:12
  319.8 0.0 copy-start
  319.8 4.9 %slice_bitcast_fusion.2 = (bf16[2048,512]{0,1:T(8,128)(2,1)}, bf16[2048,512]{0,1:T(8,128)(2,1)}) fusion(bf16[2,2048,512]{1,2,0:T(8,128)(2,1)} %all-reduce.2.cloned.1.call-done), kind=kLoop, calls=%fused_computation.46 | loop fusion | bytes 8388608 | tf_op jit(solution)/shard_map/squeeze | solution.py:70
  324.7 0.0 copy-done
  324.7 0.1 fusion.45
  324.8 0.0 copy-start.1
  324.8 10.1 %fusion.11 = f32[512,1024]{1,0:T(8,128)} fusion(bf16[2048,512]{0,1:T(8,128)(2,1)} %get-tuple-element.23, bf16[2048,512]{0,1:T(8,128)(2,1)S(1)} %fusion.45, bf16[2048,512]{0,1:T(8,128)(2,1)} %get-tuple-element.22, bf16[2048,512]{0,1:T(8,128)(2,1)} %get-tuple-element.12, bf16[2048,512]{0,1:T(8,128)(2,1)} %get-tuple-element.13), kind=kOutput, calls=%fused_computation.13 | convolution fusion | flops 4336910336 | bytes 12582912 | tf_op jit(solution)/shard_map/dot_general | solution.py:16
  334.9 0.0 copy-done.1
  334.9 0.0 copy-start.2
  334.9 9.9 %fusion.37 = f32[512,1024]{1,0:T(8,128)} fusion(f32[512,1024]{1,0:T(8,128)} %fusion.11, bf16[2048,512]{0,1:T(8,128)(2,1)S(1)} %get-tuple-element.7, bf16[2048,512]{0,1:T(8,128)(2,1)} %get-tuple-element.11, bf16[2048,512]{0,1:T(8,128)(2,1)S(1)} %copy-done.1, bf16[2048,512]{0,1:T(8,128)(2,1)} %get-tuple-element.22, bf16[2048,512]{0,1:T(8,128)(2,1)} %get-tuple-element.23), kind=kOutput, calls=%fused_computation.48 | convolution fusion | flops 4337434624 | bytes 14680064 | tf_op jit(solution)/shard_map/dot_general | solution.py:16
  344.9 0.0 reduce-scatter.2.cloned.1.call-update
  344.9 137.1 %reduce-scatter.2.cloned.1.call-done = f32[16,1024]{1,0:T(8,128)} async-done(((f32[512,1024]{1,0:T(8,128)}), f32[16,1024]{1,0:T(8,128)}) %reduce-scatter.2.cloned.1.call-update) | async-done | bytes 65552 | tf_op jit(solution)/shard_map/reduce_scatter | solution.py:89
  482.0 0.0 copy-done.2
  482.0 1.0 select_reduce_fusion.1
  483.0 0.9 add_bitcast_fusion
  483.8 0.7 copy.5
  (4 shorter events, 0.0 us)
Async XLA Ops:
  6.5 150.0 %all-gather.2.cloned.1.call-start = ((), (), s32[]{:S(2)}) async-start(), calls=%async_computation.1 | async-start | bytes 9437184 | tf_op jit(solution)/shard_map/all_gather | solution.py:30
  7.3 312.5 %all-reduce.2.cloned.1.call-start = ((), (), s32[]{:S(2)}) async-start(), calls=%async_computation.2 | async-start | bytes 8388608 | tf_op jit(solution)/shard_map/psum | solution.py:12
  119.0 18.0 %slice-start = ((s8[16777216]{0:T(1024)(128)(4,1)}), s8[4194304]{0:T(1024)(128)(4,1)S(1)}, s32[]{:S(2)}) async-start(s8[16777216]{0:T(1024)(128)(4,1)} %bitcast.32), calls=%async_computation.4 | async-start | bytes 8388608
  119.0 18.0 %slice-start.1 = ((s8[16777216]{0:T(1024)(128)(4,1)}), s8[4194304]{0:T(1024)(128)(4,1)S(1)}, s32[]{:S(2)}) async-start(s8[16777216]{0:T(1024)(128)(4,1)} %bitcast.32), calls=%async_computation.5 | async-start | bytes 8388608
  119.0 18.0 %slice-start.2 = ((s8[16777216]{0:T(1024)(128)(4,1)}), s8[4194304]{0:T(1024)(128)(4,1)S(1)}, s32[]{:S(2)}) async-start(s8[16777216]{0:T(1024)(128)(4,1)} %bitcast.32), calls=%async_computation.6 | async-start | bytes 8388608
  119.0 18.0 %slice-start.3 = ((s8[16777216]{0:T(1024)(128)(4,1)}), s8[4194304]{0:T(1024)(128)(4,1)S(1)}, s32[]{:S(2)}) async-start(s8[16777216]{0:T(1024)(128)(4,1)} %bitcast.32), calls=%async_computation.7 | async-start | bytes 8388608
  162.1 319.9 %reduce-scatter.2.cloned.1.call-start = ((), (), s32[]{:S(2)}) async-start(), calls=%async_computation.3 | async-start | bytes 2162688 | tf_op jit(solution)/shard_map/reduce_scatter | solution.py:89
  319.8 4.9 %copy-start = (bf16[2,2048,512]{1,2,0:T(8,128)(2,1)S(1)}, bf16[2,2048,512]{1,2,0:T(8,128)(2,1)}, u32[]{:S(2)}) copy-start(bf16[2,2048,512]{1,2,0:T(8,128)(2,1)} %all-reduce.2.cloned.1.call-done) | copy-start | bytes 12582916
  324.8 10.1 %copy-start.1 = (bf16[2048,512]{0,1:T(8,128)(2,1)S(1)}, bf16[2048,512]{0,1:T(8,128)(2,1)}, u32[]{:S(2)}) copy-start(bf16[2048,512]{0,1:T(8,128)(2,1)} %get-tuple-element.8) | copy-start | bytes 6291460
  334.9 147.1 %copy-start.2 = (s32[16]{0:T(128)S(1)}, s32[16]{0:T(128)}, u32[]{:S(2)}) copy-start(s32[16]{0:T(128)} %param.7) | copy-start | bytes 196
Sparse Core Ops, SparseCore 0:
  9.2 56.9 all-gather.1
  162.3 157.4 all-reduce.1
  345.0 136.9 reduce-scatter.1
where the time goes:
time: 491 us
  waiting for transfers between devices  164 us (33%)
  local copies, waits for them, and re-layouts  128 us (26%)
  matrix products  128 us (26%)
  other arithmetic  58.4 us (12%)
  between operations  13.2 us (3%)
    reduce_scatter x1, waiting for transfers between devices, body(): lax.psum_scatter(combined, ('rcv', 'src'), scatter_dimension=0, tiled=True)  137 us
    dot_general x3, matrix products, across(): lax.dot_general(first, second, (((0,), (0,)), ((), ())), precision=precis...  128 us
    unnamed x19, local copies, waits for them, and re-layouts  77.4 us
    slice x1, local copies, waits for them, and re-layouts, body(): acquired[0]  38.8 us
    select_n x1, other arithmetic, body(): jnp.where(kept_tiles[None, :, None, :, None], shaped, zero_value)  32.3 us
    psum x1, waiting for transfers between devices, broadcast(): return lax.psum(block, axis)  25.8 us
    convert_element_type x1, other arithmetic, body(): back_imag = (quarter(3, 0) + quarter(2, 1)).astype(jnp.bfloat16)  11.8 us
  transfers between devices with their start and end apart: 3, of which 2 were waited for; matrix products, arithmetic and copies ran while one was open for 57% of the time, Pallas kernels for 0%

commit v1 on v0

--- a/solution.py
+++ b/solution.py
@@ -9,7 +9,7 @@
 
 def broadcast(block, axis, holder):
     block = jnp.where(lax.axis_index(axis) == holder, block, jnp.zeros_like(block))
-    return lax.psum(block, axis)
+    return jnp.sum(lax.all_gather(block, axis), axis=0)
 
 
 def across(first, second, precision=None):

time: 491 us -> 717 us (1.46)
  waiting for transfers between devices: 164 us -> 290 us
  local copies, waits for them, and re-layouts: 128 us -> 199 us
  other arithmetic: 58.4 us -> 82.5 us
    all_gather x0 -> x1, waiting for transfers between devices: none -> 154 us  [broadcast(): return jnp.sum(lax.all_gather(block, axis), axis=0)]
    unnamed x19 -> x22, local copies, waits for them, and re-layouts: 77.4 us -> 124 us
    psum x1 -> x0, waiting for transfers between devices: 25.8 us -> none  [broadcast(): return lax.psum(block, axis)]
    slice x0 -> x2, local copies, waits for them, and re-layouts: none -> 25.1 us  [the longest x1 20.6 us: body(): green_wide = jnp.concatenate([green_block[0], green_block[1]], axis=1)]
    reduce_sum x0 -> x1, other arithmetic: none -> 11.8 us  [broadcast(): return jnp.sum(lax.all_gather(block, axis), axis=0)]
    select_n x0 -> x1, local copies, waits for them, and re-layouts: none -> 11.1 us  [broadcast(): jnp.where(lax.axis_index(axis) == holder, block, jnp.zeros_like(block))]
    squeeze x2 -> x0, local copies, waits for them, and re-layouts: 10.9 us -> none  [the longest x1 5.96 us: body(): green_wide = jnp.concatenate([green_block[0], green_block[1]], axis=1)]
    dot_general x0 -> x1, other arithmetic: none -> 7.96 us  [across(): lax.dot_general(first, second, (((0,), (0,)), ((), ())), precision=precis...]
  transfers between devices with their start and end apart: 3 -> 3, of which waited for: 2 -> 2; matrix products, arithmetic and copies ran while one was open for 57% -> 40% of each run, Pallas kernels for 0% -> 0%
where the time goes in v1:
time: 717 us; the launch traced here: 715 us
  waiting for transfers between devices  290 us (40%)
  local copies, waits for them, and re-layouts  199 us (28%)
  matrix products  130 us (18%)
  other arithmetic  82.5 us (12%)
  between operations  13.2 us (2%)
    all_gather x1, waiting for transfers between devices, broadcast(): return jnp.sum(lax.all_gather(block, axis), axis=0)  154 us
    reduce_scatter x1, waiting for transfers between devices, body(): lax.psum_scatter(combined, ('rcv', 'src'), scatter_dimension=0, tiled=True)  137 us
    dot_general x3, matrix products, across(): lax.dot_general(first, second, (((0,), (0,)), ((), ())), precision=precis...  130 us
    unnamed x22, local copies, waits for them, and re-layouts  124 us
    slice x1, local copies, waits for them, and re-layouts, body(): acquired[0]  38.6 us
    select_n x1, other arithmetic, body(): jnp.where(kept_tiles[None, :, None, :, None], shaped, zero_value)  32.4 us
    slice x1, local copies, waits for them, and re-layouts, body(): green_wide = jnp.concatenate([green_block[0], green_block[1]], axis=1)  20.6 us
  transfers between devices with their start and end apart: 3, of which 2 were waited for; matrix products, arithmetic and copies ran while one was open for 40% of the time, Pallas kernels for 0%

profile of v1, /device:TPU:0, one launch (start us, length us, event | category | flops | bytes accessed | tf_op | source)
XLA Modules:
  0.0 715.3 jit_solution(13542532985357125101)
XLA Ops:
  6.5 0.0 all-gather.4.cloned.1.call-start
  6.5 3.3 copy.14
  9.8 0.0 all-gather.4.cloned.1.call-update
  9.9 0.0 all-gather.6.cloned.1.call-start
  9.9 23.3 %copy.25 = bf16[1024,8,8,256]{3,2,1,0:T(8,128)(2,1)} copy(bf16[1024,8,8,256]{3,1,2,0:T(8,128)(2,1)} %bitcast.34) | data formatting | bytes 67108864
  33.2 0.8 compare_and_fusion
  34.0 32.4 %broadcast_select_fusion.1 = (bf16[2,16,256,8,256]{4,3,2,1,0:T(8,128)(2,1)}, bf16[2,16,256,8,256]{4,3,2,1,0:T(8,128)(2,1)}) fusion(bf16[2,16,256,8,256]{4,3,2,1,0:T(8,128)(2,1)} %bitcast.27, pred[16,8]{1,0:T(8,128)(4,1)S(1)} %get-tuple-element.10, pred[16,8]{1,0:T(8,128)(4,1)S(1)} %get-tuple-element.9), kind=kLoop, calls=%fused_computation.9 | loop fusion | flops 33554432 | bytes 100663552 | tf_op jit(solution)/shard_map/jit(_where)/select_n | solution.py:49
  66.4 38.6 %fusion.47 = (bf16[1,16,256,8,256]{4,3,2,1,0:T(8,128)(2,1)}, bf16[1,16,256,8,256]{4,3,2,1,0:T(8,128)(2,1)}, bf16[1,16,256,8,256]{4,3,2,1,0:T(8,128)(2,1)S(1)}, bf16[1,16,256,8,256]{4,3,2,1,0:T(8,128)(2,1)}) fusion(bf16[2,16,256,8,256]{4,3,2,1,0:T(8,128)(2,1)} %get-tuple-element.16, bf16[2,16,256,8,256]{4,3,2,1,0:T(8,128)(2,1)} %get-tuple-element.17), kind=kLoop, calls=%fused_computation.60 | loop fusion | bytes 134217728 | tf_op jit(solution)/shard_map/slice | solution.py:55
  105.1 16.3 %copy.26 = bf16[512,8,8,256]{3,1,2,0:T(8,128)(2,1)} copy(bf16[512,8,8,256]{3,2,1,0:T(8,128)(2,1)} %bitcast.33) | data formatting | bytes 33554432
  121.3 0.0 slice-start
  121.3 0.0 slice-start.1
  121.3 0.0 slice-start.2
  121.3 0.0 slice-start.3
  121.3 18.0 %copy.27 = bf16[512,8,8,256]{3,1,2,0:T(8,128)(2,1)} copy(bf16[512,8,8,256]{3,2,1,0:T(8,128)(2,1)} %bitcast.32) | data formatting | bytes 33554432
  139.3 0.0 slice-done
  139.3 0.0 slice-done.1
  139.4 0.0 slice-done.2
  139.4 0.0 slice-done.3
  139.4 9.7 %copy.28 = bf16[512,8,8,256]{3,1,2,0:T(8,128)(2,1)} copy(bf16[512,8,8,256]{3,2,1,0:T(8,128)(2,1)S(1)} %bitcast.31) | data formatting | bytes 33554432
  149.1 9.7 %copy.29 = bf16[512,8,8,256]{3,1,2,0:T(8,128)(2,1)} copy(bf16[512,8,8,256]{3,2,1,0:T(8,128)(2,1)S(1)} %bitcast.28) | data formatting | bytes 33554432
  158.8 0.0 all-gather.4.cloned.1.call-done
  158.8 20.6 %fusion.49 = (bf16[1,4096,512]{1,0,2:T(2,128)(2,1)}, bf16[1,4096,512]{1,0,2:T(2,128)(2,1)}) fusion(bf16[2,4096,512]{1,0,2:T(2,128)(2,1)} %all-gather.4.cloned.1.call-done), kind=kLoop, calls=%fused_computation.62 | loop fusion | bytes 16777216 | tf_op jit(solution)/shard_map/slice | solution.py:56
  179.3 18.3 %copy.21 = bf16[1,4096,512]{2,1,0:T(8,128)(2,1)} copy(bf16[1,4096,512]{1,0,2:T(2,128)(2,1)} %get-tuple-element.20) | data formatting | bytes 8388608
  197.7 18.3 %copy.22 = bf16[1,4096,512]{2,1,0:T(8,128)(2,1)} copy(bf16[1,4096,512]{1,0,2:T(2,128)(2,1)} %get-tuple-element.21) | data formatting | bytes 8388608
  216.0 7.9 %broadcast_select_fusion.2 = bf16[2,2048,512]{1,0,2:T(2,128)(2,1)} fusion(pred[]{:T(512)S(6)} %eq.26, bf16[2,4096,512]{1,0,2:T(2,128)(2,1)} %all-gather.4.cloned.1.call-done, s32[]{:T(128)S(6)} %select_n.49), kind=kLoop, calls=%fused_computation.29 | loop fusion | flops 2097152 | bytes 8388613 | tf_op jit(solution)/shard_map/jit(_where)/select_n | solution.py:11
  223.9 11.1 %copy.17 = bf16[2,2048,512]{2,1,0:T(8,128)(2,1)} copy(bf16[2,2048,512]{1,0,2:T(2,128)(2,1)} %broadcast_select_fusion.2) | data formatting | bytes 8388608 | tf_op jit(solution)/shard_map/jit(_where)/select_n | solution.py:11
  235.1 0.0 all-gather.6.cloned.1.call-update
  235.1 0.2 reduce-scatter.2.cloned.1.call-start
  235.3 8.0 %fusion.57 = bf16[4096,1024]{1,0:T(8,128)(2,1)} fusion(bf16[4096,512]{1,0:T(8,128)(2,1)} %bitcast.41, bf16[4096,512]{1,0:T(8,128)(2,1)} %bitcast.40), kind=kLoop, calls=%fused_computation.10.clone.2 | loop fusion | flops 16777216 | bytes 16777216 | tf_op jit(solution)/shard_map/dot_general | solution.py:16
  243.3 109.7 %fusion = f32[8192,1024]{0,1:T(8,128)} fusion(bf16[4096,2048]{1,0:T(8,128)(2,1)} %bitcast.38, bf16[4096,2048]{1,0:T(8,128)(2,1)} %bitcast.37, bf16[4096,2048]{1,0:T(8,128)(2,1)} %bitcast.36, bf16[4096,2048]{1,0:T(8,128)(2,1)} %bitcast.35, bf16[4096,1024]{1,0:T(8,128)(2,1)} %fusion.57), kind=kOutput, calls=%fused_computation | convolution fusion | flops 68987912192 | bytes 109051904 | tf_op jit(solution)/shard_map/dot_general | solution.py:16
  353.0 6.6 fusion.45
  359.6 11.7 %fusion.27 = (bf16[2048,512]{0,1:T(8,128)(2,1)}, bf16[2048,512]{0,1:T(8,128)(2,1)}, bf16[2048,512]{0,1:T(8,128)(2,1)}) fusion(f32[8192,1024]{0,1:T(8,128)} %fusion), kind=kLoop, calls=%fused_computation.31 | loop fusion | flops 6291456 | bytes 31457280 | tf_op jit(solution)/shard_map/convert_element_type | solution.py:68
  371.3 153.7 %all-gather.6.cloned.1.call-done = bf16[8,2048,512]{2,1,0:T(8,128)(2,1)} async-done(((bf16[2,2048,512]{2,1,0:T(8,128)(2,1)}), bf16[8,2048,512]{2,1,0:T(8,128)(2,1)}) %all-gather.6.cloned.1.call-update) | async-done | bytes 16777232 | tf_op jit(solution)/shard_map/all_gather | solution.py:12
  525.0 11.8 %reduce_sum.30 = bf16[2,2048,512]{2,1,0:T(8,128)(2,1)} reduce(bf16[4,2,2048,512]{3,2,1,0:T(8,128)(2,1)} %bitcast.39, bf16[]{:T(256)} %constant.44.clone.1), dimensions={0}, to_apply=%region_0.1 | reduce | flops 6291456 | bytes 20971522 | tf_op jit(solution)/shard_map/reduce_sum | solution.py:12
  536.8 4.5 fusion.50
  541.3 2.9 copy.24
  544.2 1.5 bitcast_negate_fusion
  545.7 3.9 copy.23
  549.6 0.0 copy-start
  549.6 10.1 %fusion.11 = f32[512,1024]{1,0:T(8,128)} fusion(bf16[2048,512]{0,1:T(8,128)(2,1)} %bitcast.44, bf16[2048,512]{0,1:T(8,128)(2,1)} %bitcast_negate_fusion, bf16[2048,512]{0,1:T(8,128)(2,1)S(1)} %bitcast.42, bf16[2048,512]{0,1:T(8,128)(2,1)} %get-tuple-element.12, bf16[2048,512]{0,1:T(8,128)(2,1)} %get-tuple-element.13), kind=kOutput, calls=%fused_computation.13 | convolution fusion | flops 4336910336 | bytes 12582912 | tf_op jit(solution)/shard_map/dot_general | solution.py:16
  559.7 0.0 copy-done
  559.7 10.0 %fusion.37 = f32[512,1024]{1,0:T(8,128)} fusion(f32[512,1024]{1,0:T(8,128)} %fusion.11, bf16[2048,512]{0,1:T(8,128)(2,1)} %get-tuple-element.7, bf16[2048,512]{0,1:T(8,128)(2,1)} %get-tuple-element.11, bf16[2048,512]{0,1:T(8,128)(2,1)} %get-tuple-element.8, bf16[2048,512]{0,1:T(8,128)(2,1)S(1)} %bitcast.43, bf16[2048,512]{0,1:T(8,128)(2,1)S(1)} %bitcast.45), kind=kOutput, calls=%fused_computation.44 | convolution fusion | flops 4337434624 | bytes 14680064 | tf_op jit(solution)/shard_map/dot_general | solution.py:16
  569.7 0.0 reduce-scatter.2.cloned.1.call-update
  569.7 136.6 %reduce-scatter.2.cloned.1.call-done = f32[16,1024]{1,0:T(8,128)} async-done(((f32[512,1024]{1,0:T(8,128)}), f32[16,1024]{1,0:T(8,128)}) %reduce-scatter.2.cloned.1.call-update) | async-done | bytes 65552 | tf_op jit(solution)/shard_map/reduce_scatter | solution.py:89
  706.3 0.0 copy-done.1
  706.3 1.0 select_reduce_fusion.1
  707.2 0.9 add_bitcast_fusion
  708.1 0.7 copy.19
  (5 shorter events, 0.0 us)
Async XLA Ops:
  6.5 152.2 %all-gather.4.cloned.1.call-start = ((), (), s32[]{:S(2)}) async-start(), calls=%async_computation.1 | async-start | bytes 9437184 | tf_op jit(solution)/shard_map/all_gather | solution.py:30
  9.9 515.1 %all-gather.6.cloned.1.call-start = ((), (), s32[]{:S(2)}) async-start(), calls=%async_computation.3 | async-start | bytes 20971520 | tf_op jit(solution)/shard_map/all_gather | solution.py:12
  121.3 18.0 %slice-start = ((s8[16777216]{0:T(1024)(128)(4,1)}), s8[4194304]{0:T(1024)(128)(4,1)S(1)}, s32[]{:S(2)}) async-start(s8[16777216]{0:T(1024)(128)(4,1)} %bitcast.29), calls=%async_computation.4 | async-start | bytes 8388608
  121.3 18.0 %slice-start.1 = ((s8[16777216]{0:T(1024)(128)(4,1)}), s8[4194304]{0:T(1024)(128)(4,1)S(1)}, s32[]{:S(2)}) async-start(s8[16777216]{0:T(1024)(128)(4,1)} %bitcast.29), calls=%async_computation.5 | async-start | bytes 8388608
  121.3 18.0 %slice-start.2 = ((s8[16777216]{0:T(1024)(128)(4,1)}), s8[4194304]{0:T(1024)(128)(4,1)S(1)}, s32[]{:S(2)}) async-start(s8[16777216]{0:T(1024)(128)(4,1)} %bitcast.29), calls=%async_computation.6 | async-start | bytes 8388608
  121.3 18.0 %slice-start.3 = ((s8[16777216]{0:T(1024)(128)(4,1)}), s8[4194304]{0:T(1024)(128)(4,1)S(1)}, s32[]{:S(2)}) async-start(s8[16777216]{0:T(1024)(128)(4,1)} %bitcast.29), calls=%async_computation.7 | async-start | bytes 8388608
  235.1 471.2 %reduce-scatter.2.cloned.1.call-start = ((), (), s32[]{:S(2)}) async-start(), calls=%async_computation.2 | async-start | bytes 2162688 | tf_op jit(solution)/shard_map/reduce_scatter | solution.py:89
  549.6 10.1 %copy-start = (bf16[1,2048,512]{1,2,0:T(8,128)(2,1)S(1)}, bf16[1,2048,512]{1,2,0:T(8,128)(2,1)}, u32[]{:S(2)}) copy-start(bf16[1,2048,512]{1,2,0:T(8,128)(2,1)} %copy.23) | copy-start | bytes 6291460
  559.7 146.6 %copy-start.1 = (s32[16]{0:T(128)S(1)}, s32[16]{0:T(128)}, u32[]{:S(2)}) copy-start(s32[16]{0:T(128)} %param.7) | copy-start | bytes 196
Sparse Core Ops, SparseCore 0:
  10.0 56.9 all-gather.3
  235.2 289.7 all-gather.5
  569.8 136.4 reduce-scatter.1
